TPU v7x, 512 devices: a whole 4x4x16 slice. The times are simulated.
512 devices in a mesh: row: 16 (over x_hi, y, core), col: 32 (over x_lo, z).
Axes of the slice: x: 4 (x_hi: 2, x_lo: 2; x = x_hi * 2 + x_lo), y: 4, z: 16, core: 2. Of those that a mesh axis runs over, the one named last changes fastest.
Arguments:
- blocks: bfloat16 [1536, 64, 4096], P('col', 'row'), may hold values from -1.75 to 1.75
- columns: int32 [1536, 64], P('col', 'row'), may hold values from 0 to 95, as said below
- counts: int32 [1536, 16], P('col', 'row'), may hold values from 0 to 4, as said below
Outputs:
- product: bfloat16 [1536, 64, 4096], P('col', 'row')
Inputs may be any that keep to these rules, and one draw needn't show every extreme that they name: `counts`: in each tile, every block row has between 0 and 4 live slots; in every tile some block row has exactly 4. The live slots of a block row name different tile columns, at most 2 of them below 48 and at most 2 at or above; in every tile some block row reaches 2 in both halves. A live tile column t of global block row g satisfies (t - g) mod 48 < 8. Dead slots hold arbitrary values in the range.
All inputs are finite; a program needn't handle non-finite values.
Results may differ from a plain program's by a relative error of at most 0.001.
Values may be sent and summed in bfloat16 or wider, within the bound.
No kernel may reach another device: no remote copies, remote signals or barrier semaphores. Data moves between devices by JAX's collectives and lax.ppermute only.
A program may use at most 128 MiB of HBM per device.

v0:
```python
import jax
import jax.numpy as jnp
from jax import lax
from jax.sharding import PartitionSpec as P

BLK = 64
HS = 2
SECTIONS = 2


def broadcast(block, axis, owner):
    block = jnp.where(lax.axis_index(axis) == owner, block, jnp.zeros_like(block))
    return lax.psum(block, axis)


def from_behind(block, axis, distance):
    devices = range(lax.axis_size(axis))
    route = [((i - distance) % len(devices), i) for i in devices]
    return lax.ppermute(block, axis, route)


def compact(tile_blocks, tile_cols, tile_count, half_index):
    strip_count = tile_cols.shape[0]
    slot_count = tile_cols.shape[1]
    slot_ids = jnp.arange(slot_count, dtype=jnp.int32)
    live_slots = (slot_ids[None, :] < tile_count[:, None]) & (
        tile_cols // strip_count == half_index
    )
    position = jnp.cumsum(live_slots.astype(jnp.int32), axis=1) - 1
    chosen = live_slots[:, :, None] & (
        position[:, :, None] == jnp.arange(HS, dtype=jnp.int32)[None, None, :]
    )
    picked = jnp.einsum(
        "isq,isx->iqx",
        chosen.astype(jnp.bfloat16),
        tile_blocks,
        preferred_element_type=jnp.bfloat16,
    )
    inner_rows = jnp.sum(
        jnp.where(chosen, (tile_cols - half_index * strip_count)[:, :, None], 0), axis=1
    ).astype(jnp.int32)
    used_flags = jnp.any(chosen, axis=1).astype(jnp.int32)
    return (picked, inner_rows, used_flags)


def section_term(
    picked, inner_rows, used_flags, right_blocks, right_cols, right_count, out_cols, out_live
):
    strip_count = picked.shape[0]
    slot_count = out_cols.shape[1]
    gathered = right_blocks[inner_rows]
    gathered_cols = right_cols[inner_rows]
    gathered_count = right_count[inner_rows]
    slot_ids = jnp.arange(slot_count, dtype=jnp.int32)
    right_live = slot_ids[None, None, :] < gathered_count[:, :, None]
    matches = (gathered_cols[:, :, :, None] == out_cols[:, None, None, :]) & right_live[
        :, :, :, None
    ]
    matches = matches & (used_flags[:, :, None, None] > 0) & out_live[:, None, None, :]
    selected = jnp.einsum(
        "iqbj,iqbx->iqjx",
        matches.astype(jnp.bfloat16),
        gathered,
        preferred_element_type=jnp.bfloat16,
    )
    left_blocks = picked.reshape(strip_count, HS, BLK, BLK)
    right_sel = selected.reshape(strip_count, HS, slot_count, BLK, BLK)
    contribution = jnp.einsum(
        "iqmn,iqjnp->ijmp", left_blocks, right_sel, preferred_element_type=jnp.float32
    )
    return contribution.reshape(strip_count, slot_count, BLK * BLK)


def local(blocks, columns, counts):
    count_now = counts[:, 0]
    strip_count = columns.shape[0]
    slot_count = columns.shape[1]
    out_live = jnp.arange(slot_count, dtype=jnp.int32)[None, :] < count_now[:, None]
    col_index = lax.axis_index("col")
    col_total = lax.axis_size("col")
    accumulated = jnp.zeros((strip_count, slot_count, blocks.shape[2]), jnp.float32)
    right_tile = (blocks, columns, count_now)
    for section in range(SECTIONS):
        target_piece = (col_index + section) % col_total
        root_index = target_piece // 2
        half_index = target_piece % 2
        got_blocks, got_cols, got_count = (
            broadcast(blocks, "row", root_index),
            broadcast(columns, "row", root_index),
            broadcast(count_now, "row", root_index),
        )
        picked, inner_rows, used_flags = compact(got_blocks, got_cols, got_count, half_index)
        if section > 0:
            right_tile = from_behind((right_tile[0], right_tile[1], right_tile[2]), "col", -1)
        accumulated = accumulated + section_term(
            picked,
            inner_rows,
            used_flags,
            right_tile[0],
            right_tile[1],
            right_tile[2],
            columns,
            out_live,
        )
    return accumulated.astype(jnp.bfloat16)


def solution(mesh):
    return jax.shard_map(
        local,
        mesh=mesh,
        in_specs=(P("col", "row", None), P("col", "row"), P("col", "row")),
        out_specs=P("col", "row", None),
        check_vma=False,
    )
```

profile of v0, /device:TPU:1, one launch (start us, length us, event | category | flops | bytes accessed | tf_op | source)
XLA Modules:
  0.0 228.3 jit_solution(16284222606765548050)
XLA Ops:
  6.5 12.9 %collective-permute-start.2 = (bf16[48,4,4096]{2,1,0:T(4,128)(2,1)}, bf16[48,4,4096]{2,1,0:T(4,128)(2,1)S(1)}, u32[]{:S(2)}, u32[]{:S(2)}) collective-permute-start(bf16[48,4,4096]{2,1,0:T(4,128)(2,1)} %param.3), channel_id=1, source_target_pairs={{1,0},{2,1},{3,2},{4,3},{5,4},{6,5},{7,6},{8,7},{9,8},{10,9},{11,1... | collective-permute-start | bytes 4718600 | tf_op jit(solution)/shard_map/ppermute | solution.py:19
  20.2 2.6 %collective-permute-start = (s32[48,4]{1,0:T(8,128)S(1)}, s32[48,4]{1,0:T(8,128)S(1)}, u32[]{:S(2)}, u32[]{:S(2)}) collective-permute-start(s32[48,4]{1,0:T(8,128)S(1)} %copy.37), channel_id=1, source_target_pairs={{1,0},{2,1},{3,2},{4,3},{5,4},{6,5},{7,6},{8,7},{9,8},{10,9},{11,1... | collective-permute-start | bytes 2312 | tf_op jit(solution)/shard_map/ppermute | solution.py:19
  22.8 2.6 %collective-permute-start.1 = (s32[48]{0:T(128)}, s32[48]{0:T(128)S(1)}, u32[]{:S(2)}, u32[]{:S(2)}) collective-permute-start(s32[48]{0:T(128)} %bitcast.53), channel_id=1, source_target_pairs={{1,0},{2,1},{3,2},{4,3},{5,4},{6,5},{7,6},{8,7},{9,8},{10,9},{11,1... | collective-permute-start | bytes 584 | tf_op jit(solution)/shard_map/ppermute | solution.py:19
  25.6 4.4 %broadcast_select_fusion = (bf16[48,4,4096]{2,1,0:T(4,128)(2,1)}, bf16[48,4,4096]{2,1,0:T(4,128)(2,1)}) fusion(bf16[48,4,4096]{2,1,0:T(4,128)(2,1)} %param.3, pred[]{:T(512)S(6)} %eq.86, pred[]{:T(512)S(6)} %eq.39), kind=kLoop, calls=%fused_computation.12 | loop fusion | flops 1572864 | bytes 4718594 | tf_op jit(solution)/shard_map/jit(_where)/select_n | solution.py:12
  30.0 12.7 %all-reduce = (s32[48,4]{0,1:T(4,128)S(1)}, s32[48]{0:T(128)S(1)}, s32[48,4]{0,1:T(4,128)S(1)}, s32[48]{0:T(128)S(1)}) all-reduce(s32[48,4]{0,1:T(4,128)S(1)} %get-tuple-element.22, s32[48]{0:T(128)S(1)} %get-tuple-element.24, s32[48,4]{0,1:T(4,128)S(1)} %get-tuple-element.21, ...), channel_id=1, replica_groups=mesh['row'=16,'col'=32] {'row'}, use_global_device_ids=true, to_apply=%region_1.2 | all-reduce | flops 480 | bytes 3840 | tf_op jit(solution)/shard_map/psum | solution.py:13
  43.4 1.7 fusion.31
  45.1 0.9 select_reduce_fusion.1
  46.3 7.4 %gather_fusion.2 = bf16[96,4,4096]{2,1,0:T(4,128)(2,1)} fusion(bf16[48,4,4096]{2,1,0:T(4,128)(2,1)S(1)} %copy-done.1, s32[1024]{0:T(1024)S(1)} %pad_clamp_fusion.1), kind=kCustom, calls=%fused_computation.2 | custom fusion | bytes 6291840 | tf_op jit(solution)/shard_map/gather | solution.py:51
  54.3 1.2 gather_fusion.1
  57.2 5.5 %fusion.10 = bf16[48,2,4,4096]{3,2,1,0:T(4,128)(2,1)} fusion(bf16[48,2,4,4096]{3,2,1,0:T(4,128)(2,1)} %bitcast.58, s32[48,4]{1,0:T(8,128)S(1)} %copy.37, s32[48,2,4]{2,1,0:T(2,128)S(1)} %bitcast.60, pred[48,4]{1,0:T(8,128)(4,1)S(1)} %iota_compare_fusion.2, pred[48,2]{1,0:T(8,128)(4,1)S(1)} %convert_compare_fusion.1, ...), kind=kOutput, calls=%fused_computation.19 | convolution fusion | flops 12589056 | bytes 6294432 | tf_op jit(solution)/shard_map/iqbj,iqbx->iqjx/dot_general | solution.py:60
  62.7 10.0 %reshape.101 = bf16[48,2,4,64,64]{4,3,2,1,0:T(8,128)(2,1)} reshape(bf16[48,2,4,4096]{3,2,1,0:T(4,128)(2,1)} %fusion.10) | data formatting | bytes 6291456 | tf_op jit(solution)/shard_map/reshape | solution.py:67
  72.7 1.2 gather_fusion.4
  74.9 7.3 %gather_fusion.5 = bf16[96,4,4096]{2,1,0:T(4,128)(2,1)} fusion(bf16[48,4,4096]{2,1,0:T(4,128)(2,1)S(1)} %collective-permute-done.2, s32[1024]{0:T(1024)S(1)} %pad_clamp_fusion), kind=kCustom, calls=%fused_computation.5 | custom fusion | bytes 6291840 | tf_op jit(solution)/shard_map/gather | solution.py:51
  82.1 5.5 %fusion.5 = bf16[48,2,4,4096]{3,2,1,0:T(4,128)(2,1)} fusion(bf16[48,2,4,4096]{3,2,1,0:T(4,128)(2,1)} %bitcast.59, s32[48,2,4]{2,1,0:T(2,128)S(1)} %bitcast.61, s32[48,4]{1,0:T(8,128)S(1)} %copy.37, pred[48,2]{1,0:T(8,128)(4,1)S(1)} %convert_compare_fusion, pred[48,2,4]{2,1,0:T(4,128)(4,1)S(1)} %iota_compare_fusion, pred[48,4]{1,0:T(8,128)(4,1)S(1)} %iota_compare_fusion.2), kind=kOutput, calls=%fused_computation.14 | convolution fusion | flops 12589056 | bytes 6294432 | tf_op jit(solution)/shard_map/iqbj,iqbx->iqjx/dot_general | solution.py:60
  87.6 10.0 %reshape.103 = bf16[48,2,4,64,64]{4,3,2,1,0:T(8,128)(2,1)} reshape(bf16[48,2,4,4096]{3,2,1,0:T(4,128)(2,1)} %fusion.5) | data formatting | bytes 6291456 | tf_op jit(solution)/shard_map/reshape | solution.py:67
  97.6 94.2 %all-reduce.4.cloned.1.call-done = (bf16[48,4,4096]{2,1,0:T(4,128)(2,1)}, bf16[48,4,4096]{2,1,0:T(4,128)(2,1)}) async-done(((bf16[48,4,4096]{2,1,0:T(4,128)(2,1)}, bf16[48,4,4096]{2,1,0:T(4,128)(2,1)}), (bf16[48,4,4096]{2,1,0:T(4,128)(2,1)}, bf16[48,4,4096]{2,1,0:T(4,128)(2,1)})) %all-reduce.4.cloned.1.call-update) | async-done | bytes 3145744 | tf_op jit(solution)/shard_map/psum | solution.py:13
  191.8 2.4 %fusion.37 = bf16[48,2,4096]{2,1,0:T(2,128)(2,1)S(1)} fusion(pred[48,4,2]{1,2,0:T(4,128)(4,1)S(1)} %get-tuple-element.26, bf16[48,4,4096]{2,1,0:T(4,128)(2,1)} %get-tuple-element.9), kind=kOutput, calls=%fused_computation.73 | convolution fusion | flops 3145728 | bytes 2359680 | tf_op jit(solution)/shard_map/isq,isx->iqx/dot_general | solution.py:33
  194.2 1.9 reshape.159
  196.1 2.4 %fusion.38 = bf16[48,2,4096]{2,1,0:T(2,128)(2,1)S(1)} fusion(pred[48,4,2]{1,2,0:T(4,128)(4,1)S(1)} %get-tuple-element.12, bf16[48,4,4096]{2,1,0:T(4,128)(2,1)} %get-tuple-element.10), kind=kOutput, calls=%fused_computation.74 | convolution fusion | flops 3145728 | bytes 2359680 | tf_op jit(solution)/shard_map/isq,isx->iqx/dot_general | solution.py:33
  198.5 1.9 reshape.161
  200.4 7.8 %fusion.3 = f32[48,4,64,64,1]{3,2,1,4,0:T(8,128)} fusion(bf16[48,2,4,64,64]{4,3,2,1,0:T(8,128)(2,1)} %reshape.101, bf16[48,2,64,64,1]{3,2,1,0,4:T(8,128)(2,1)} %reshape.159), kind=kOutput, calls=%fused_computation.10 | convolution fusion | flops 201326592 | bytes 7077888 | tf_op jit(solution)/shard_map/iqmn,iqjnp->ijmp/dot_general | solution.py:68
  208.3 6.5 %fusion.1 = bf16[48,4,64,64]{2,3,1,0:T(8,128)(2,1)} fusion(f32[48,4,64,64,1]{3,2,1,4,0:T(8,128)} %fusion.3, bf16[48,2,4,64,64]{4,3,2,1,0:T(8,128)(2,1)S(1)} %bitcast.57, bf16[48,2,64,64,1]{3,2,1,0,4:T(8,128)(2,1)S(1)} %copy-done.2), kind=kOutput, calls=%fused_computation.8 | convolution fusion | flops 202899456 | bytes 8650752 | tf_op jit(solution)/shard_map/iqmn,iqjnp->ijmp/dot_general | solution.py:68
  214.8 3.4 %copy.57 = bf16[48,4,64,64]{3,2,1,0:T(8,128)(2,1)S(1)} copy(bf16[48,4,64,64]{2,3,1,0:T(8,128)(2,1)} %fusion.1) | data formatting | bytes 3145728 | tf_op jit(solution)/shard_map/convert_element_type | solution.py:105
  218.2 3.2 %reshape.165 = bf16[48,4,4096]{2,1,0:T(4,128)(2,1)} reshape(bf16[48,4,64,64]{3,2,1,0:T(8,128)(2,1)S(1)} %copy.57) | data formatting | bytes 3145728 | tf_op jit(solution)/shard_map/convert_element_type | solution.py:105
  (54 shorter events, 4.9 us)
Async XLA Ops:
  6.5 185.3 %all-reduce.4.cloned.1.call-start = ((), (), s32[]{:S(2)}) async-start(), calls=%async_computation | async-start | bytes 6291456 | tf_op jit(solution)/shard_map/psum | solution.py:13
  6.5 68.3 %collective-permute-start.2 = (bf16[48,4,4096]{2,1,0:T(4,128)(2,1)}, bf16[48,4,4096]{2,1,0:T(4,128)(2,1)S(1)}, u32[]{:S(2)}, u32[]{:S(2)}) collective-permute-start(bf16[48,4,4096]{2,1,0:T(4,128)(2,1)} %param.3), channel_id=1, source_target_pairs={{1,0},{2,1},{3,2},{4,3},{5,4},{6,5},{7,6},{8,7},{9,8},{10,9},{11,1... | collective-permute-start | bytes 4718600 | tf_op jit(solution)/shard_map/ppermute | solution.py:19
  20.2 54.0 %collective-permute-start = (s32[48,4]{1,0:T(8,128)S(1)}, s32[48,4]{1,0:T(8,128)S(1)}, u32[]{:S(2)}, u32[]{:S(2)}) collective-permute-start(s32[48,4]{1,0:T(8,128)S(1)} %copy.37), channel_id=1, source_target_pairs={{1,0},{2,1},{3,2},{4,3},{5,4},{6,5},{7,6},{8,7},{9,8},{10,9},{11,1... | collective-permute-start | bytes 2312 | tf_op jit(solution)/shard_map/ppermute | solution.py:19
  22.8 49.9 %collective-permute-start.1 = (s32[48]{0:T(128)}, s32[48]{0:T(128)S(1)}, u32[]{:S(2)}, u32[]{:S(2)}) collective-permute-start(s32[48]{0:T(128)} %bitcast.53), channel_id=1, source_target_pairs={{1,0},{2,1},{3,2},{4,3},{5,4},{6,5},{7,6},{8,7},{9,8},{10,9},{11,1... | collective-permute-start | bytes 584 | tf_op jit(solution)/shard_map/ppermute | solution.py:19
  25.5 4.4 %copy-start = (s32[48,1]{0,1:T(1,128)S(1)}, s32[48,1]{0,1:T(1,128)}, u32[]{:S(2)}) copy-start(s32[48,1]{0,1:T(1,128)} %param.5) | copy-start | bytes 580
  25.5 4.4 %copy-start.3 = (s32[48,4]{0,1:T(4,128)S(1)}, s32[48,4]{0,1:T(4,128)}, u32[]{:S(2)}) copy-start(s32[48,4]{0,1:T(4,128)} %param.4) | copy-start | bytes 2308
  25.6 20.8 %copy-start.1 = (bf16[48,4,4096]{2,1,0:T(4,128)(2,1)S(1)}, bf16[48,4,4096]{2,1,0:T(4,128)(2,1)}, u32[]{:S(2)}) copy-start(bf16[48,4,4096]{2,1,0:T(4,128)(2,1)} %param.3) | copy-start | bytes 4718596
  198.5 9.8 %slice-start = ((s8[6291456]{0:T(1024)(128)(4,1)}), s8[2097152]{0:T(1024)(128)(4,1)S(1)}, s32[]{:S(2)}) async-start(s8[6291456]{0:T(1024)(128)(4,1)} %bitcast.56), calls=%async_computation.1 | async-start | bytes 4194304
  200.4 7.9 %slice-start.1 = ((s8[6291456]{0:T(1024)(128)(4,1)}), s8[4194304]{0:T(1024)(128)(4,1)S(1)}, s32[]{:S(2)}) async-start(s8[6291456]{0:T(1024)(128)(4,1)} %bitcast.56), calls=%async_computation.2 | async-start | bytes 8388608
  200.4 7.9 %copy-start.2 = (bf16[48,2,64,64,1]{3,2,1,0,4:T(8,128)(2,1)S(1)}, bf16[48,2,64,64,1]{3,2,1,0,4:T(8,128)(2,1)}, u32[]{:S(2)}) copy-start(bf16[48,2,64,64,1]{3,2,1,0,4:T(8,128)(2,1)} %reshape.161) | copy-start | bytes 2359300
Sparse Core Ops, SparseCore 0:
  30.1 161.6 all-reduce.3
where the time goes:
time: 229 us; the launch traced here: 228 us
  waiting for transfers between devices  94.2 us (41%)
  local copies, waits for them, and re-layouts  51 us (22%)
  matrix products  30.1 us (13%)
  starting transfers between devices  18.1 us (8%)
  between operations  13.7 us (6%)
  blocking collectives  12.7 us (6%)
  other arithmetic  8.37 us (4%)
    psum x1, waiting for transfers between devices, broadcast(): return lax.psum(block, axis)  94.2 us
    reshape x2, local copies, waits for them, and re-layouts, section_term(): right_sel = selected.reshape(strip_count, HS, slot_count, BLK, BLK)  20 us
    ppermute x3, starting transfers between devices, from_behind(): return lax.ppermute(block, axis, route)  18.1 us
    gather x2, local copies, waits for them, and re-layouts, section_term(): gathered = right_blocks[inner_rows]  14.6 us
    dot_general x2, matrix products, section_term(): jnp.einsum('iqmn,iqjnp->ijmp', left_blocks, right_sel, preferred_element_...  14.4 us
    psum x1, blocking collectives, broadcast(): return lax.psum(block, axis)  12.7 us
    dot_general x2, matrix products, section_term(): jnp.einsum('iqbj,iqbx->iqjx', matches.astype(jnp.bfloat16), gathered, pre...  11 us
    convert_element_type x2, local copies, waits for them, and re-layouts, local(): return accumulated.astype(jnp.bfloat16)  6.61 us
  transfers between devices with their start and end apart: 4, of which 1 were waited for; matrix products, arithmetic and copies ran while one was open for 26% of the time, Pallas kernels for 0%

commit v1 on v0

--- a/solution.py
+++ b/solution.py
@@ -8,9 +8,15 @@
 SECTIONS = 2
 
 
+def add_all(x, mesh_axis):
+    shards = lax.all_gather(x, mesh_axis, axis=0, tiled=False)
+    total = shards.sum(axis=0)
+    return total
+
+
 def broadcast(block, axis, owner):
     block = jnp.where(lax.axis_index(axis) == owner, block, jnp.zeros_like(block))
-    return lax.psum(block, axis)
+    return add_all(block, axis)
 
 
 def from_behind(block, axis, distance):

time: 229 us -> 409 us (1.79)
  waiting for transfers between devices: 94.2 us -> 202 us
  blocking collectives: 12.7 us -> 55.9 us
  other arithmetic: 8.37 us -> 35.6 us
    all_gather x0 -> x2, waiting for transfers between devices: none -> 202 us  [add_all(): shards = lax.all_gather(x, mesh_axis, axis=0, tiled=False)]
    psum x1 -> x0, waiting for transfers between devices: 94.2 us -> none  [broadcast(): return lax.psum(block, axis)]
    all_gather x0 -> x2, blocking collectives: none -> 42.5 us  [add_all(): shards = lax.all_gather(x, mesh_axis, axis=0, tiled=False)]
    reduce_sum x0 -> x6, other arithmetic: none -> 26.9 us  [add_all(): total = shards.sum(axis=0)]
    unnamed x0 -> x1, blocking collectives: none -> 13.4 us
    psum x1 -> x0, blocking collectives: 12.7 us -> none  [broadcast(): return lax.psum(block, axis)]
  transfers between devices with their start and end apart: 4 -> 5, of which waited for: 1 -> 2; matrix products, arithmetic and copies ran while one was open for 26% -> 17% of each run, Pallas kernels for 0% -> 0%
where the time goes in v1:
time: 409 us; the launch traced here: 408 us
  waiting for transfers between devices  202 us (49%)
  blocking collectives  55.9 us (14%)
  local copies, waits for them, and re-layouts  53.4 us (13%)
  other arithmetic  35.6 us (9%)
  matrix products  28.4 us (7%)
  starting transfers between devices  18.2 us (4%)
  between operations  14.3 us (3%)
    all_gather x2, waiting for transfers between devices, add_all(): shards = lax.all_gather(x, mesh_axis, axis=0, tiled=False)  202 us
    all_gather x2, blocking collectives, add_all(): shards = lax.all_gather(x, mesh_axis, axis=0, tiled=False)  42.5 us
    reduce_sum x6, other arithmetic, add_all(): total = shards.sum(axis=0)  26.9 us
    reshape x2, local copies, waits for them, and re-layouts, section_term(): right_sel = selected.reshape(strip_count, HS, slot_count, BLK, BLK)  20.2 us
    ppermute x3, starting transfers between devices, from_behind(): return lax.ppermute(block, axis, route)  18.1 us
    dot_general x2, matrix products, section_term(): jnp.einsum('iqmn,iqjnp->ijmp', left_blocks, right_sel, preferred_element_...  14.5 us
    gather x2, local copies, waits for them, and re-layouts, section_term(): gathered = right_blocks[inner_rows]  14.3 us
    unnamed x1, blocking collectives  13.4 us
  transfers between devices with their start and end apart: 5, of which 2 were waited for; matrix products, arithmetic and copies ran while one was open for 17% of the time, Pallas kernels for 0%

profile of v1, /device:TPU:1, one launch (start us, length us, event | category | flops | bytes accessed | tf_op | source)
XLA Modules:
  0.0 408.0 jit_solution(419938740897597998)
XLA Ops:
  6.5 4.4 %broadcast_select_fusion = (bf16[48,4,4096]{2,1,0:T(4,128)(2,1)}, bf16[48,4,4096]{2,1,0:T(4,128)(2,1)}) fusion(bf16[48,4,4096]{2,1,0:T(4,128)(2,1)} %param.3, pred[]{:T(512)S(6)} %eq.102, pred[]{:T(512)S(6)} %eq.93), kind=kLoop, calls=%fused_computation.12 | loop fusion | flops 1572864 | bytes 4718594 | tf_op jit(solution)/shard_map/jit(_where)/select_n | solution.py:18
  11.7 12.9 %collective-permute-start.2 = (bf16[48,4,4096]{2,1,0:T(4,128)(2,1)S(1)}, bf16[48,4,4096]{2,1,0:T(4,128)(2,1)S(1)}, u32[]{:S(2)}, u32[]{:S(2)}) collective-permute-start(bf16[48,4,4096]{2,1,0:T(4,128)(2,1)S(1)} %copy-done.1), channel_id=1, source_target_pairs={{1,0},{2,1},{3,2},{4,3},{5,4},{6,5},{7,6},{8,7},{9,8},{10,9},{11,1... | collective-permute-start | bytes 4718600 | tf_op jit(solution)/shard_map/ppermute | solution.py:25
  24.6 2.6 collective-permute-start.1
  27.3 2.6 collective-permute-start
  32.1 13.4 %all-reduce.2 = (s32[768]{0:T(1024)S(1)}, s32[768]{0:T(1024)S(1)}) all-reduce(s32[768]{0:T(1024)S(1)} %fusion.32, s32[768]{0:T(1024)S(1)} %fusion.34), channel_id=2, replica_groups=mesh['row'=16,'col'=32] {'row'}, use_global_device_ids=true, to_apply=%add | all-reduce | flops 1536 | bytes 12288
  45.6 22.4 %all-gather.6 = s32[16,48,4]{1,2,0:T(4,128)S(1)} all-gather(s32[1,48,4]{1,2,0:T(4,128)S(1)} %get-tuple-element.18), channel_id=3, replica_groups=mesh['row'=16,'col'=32] {'row'}, dimensions={0}, use_global_device_ids=true | all-gather | bytes 13056 | tf_op jit(solution)/shard_map/all_gather | solution.py:12
  72.4 7.2 %gather_fusion.2 = bf16[96,4,4096]{2,1,0:T(4,128)(2,1)} fusion(bf16[48,4,4096]{2,1,0:T(4,128)(2,1)S(1)} %copy-done.1, s32[1024]{0:T(1024)S(1)} %pad_clamp_fusion.1), kind=kCustom, calls=%fused_computation.2 | custom fusion | bytes 6291840 | tf_op jit(solution)/shard_map/gather | solution.py:57
  79.6 20.1 %all-gather.7 = s32[16,48,4]{1,2,0:T(4,128)S(1)} all-gather(s32[1,48,4]{1,2,0:T(4,128)S(1)} %get-tuple-element.17), channel_id=6, replica_groups=mesh['row'=16,'col'=32] {'row'}, dimensions={0}, use_global_device_ids=true | all-gather | bytes 13056 | tf_op jit(solution)/shard_map/all_gather | solution.py:12
  102.6 5.7 %fusion.10 = bf16[48,2,4,4096]{3,2,1,0:T(4,128)(2,1)} fusion(bf16[48,2,4,4096]{3,2,1,0:T(4,128)(2,1)} %bitcast.73, s32[48,4]{1,0:T(8,128)S(1)} %copy.54, s32[48,2,4]{2,1,0:T(2,128)S(1)} %bitcast.75, pred[48,4]{1,0:T(8,128)(4,1)S(1)} %iota_compare_fusion.2, pred[48,2]{1,0:T(8,128)(4,1)S(1)} %convert_compare_fusion.1, ...), kind=kOutput, calls=%fused_computation.19 | convolution fusion | flops 12589056 | bytes 6294432 | tf_op jit(solution)/shard_map/iqbj,iqbx->iqjx/dot_general | solution.py:66
  108.3 10.2 %reshape.251 = bf16[48,2,4,64,64]{4,3,2,1,0:T(8,128)(2,1)} reshape(bf16[48,2,4,4096]{3,2,1,0:T(4,128)(2,1)} %fusion.10) | data formatting | bytes 6291456 | tf_op jit(solution)/shard_map/reshape | solution.py:73
  120.6 7.2 %gather_fusion.5 = bf16[96,4,4096]{2,1,0:T(4,128)(2,1)} fusion(bf16[48,4,4096]{2,1,0:T(4,128)(2,1)S(1)} %collective-permute-done.2, s32[1024]{0:T(1024)S(1)} %pad_clamp_fusion), kind=kCustom, calls=%fused_computation.5 | custom fusion | bytes 6291840 | tf_op jit(solution)/shard_map/gather | solution.py:57
  127.8 5.4 %fusion.5 = bf16[48,2,4,4096]{3,2,1,0:T(4,128)(2,1)} fusion(bf16[48,2,4,4096]{3,2,1,0:T(4,128)(2,1)} %bitcast.74, s32[48,2,4]{2,1,0:T(2,128)S(1)} %bitcast.76, s32[48,4]{1,0:T(8,128)S(1)} %copy.54, pred[48,2]{1,0:T(8,128)(4,1)S(1)} %convert_compare_fusion, pred[48,2,4]{2,1,0:T(4,128)(4,1)S(1)} %iota_compare_fusion, pred[48,4]{1,0:T(8,128)(4,1)S(1)} %iota_compare_fusion.2), kind=kOutput, calls=%fused_computation.14 | convolution fusion | flops 12589056 | bytes 6294432 | tf_op jit(solution)/shard_map/iqbj,iqbx->iqjx/dot_general | solution.py:66
  133.2 10.0 %reshape.253 = bf16[48,2,4,64,64]{4,3,2,1,0:T(8,128)(2,1)} reshape(bf16[48,2,4,4096]{3,2,1,0:T(4,128)(2,1)} %fusion.5) | data formatting | bytes 6291456 | tf_op jit(solution)/shard_map/reshape | solution.py:73
  143.2 51.8 %all-gather.13.cloned.1.call-done = bf16[768,4,4096]{2,1,0:T(4,128)(2,1)} async-done(((bf16[48,4,4096]{2,1,0:T(4,128)(2,1)}), bf16[768,4,4096]{2,1,0:T(4,128)(2,1)}) %all-gather.13.cloned.1.call-update) | async-done | bytes 25165840 | tf_op jit(solution)/shard_map/all_gather | solution.py:12
  195.0 13.3 %reduce_sum.91 = bf16[48,4,4096]{2,1,0:T(4,128)(2,1)S(1)} reduce(bf16[16,48,4,4096]{3,2,1,0:T(4,128)(2,1)} %bitcast.69, bf16[]{:T(256)} %constant.89.clone.1), dimensions={0}, to_apply=%region_11.12 | reduce | flops 11796480 | bytes 26738690 | tf_op jit(solution)/shard_map/reduce_sum | solution.py:13
  209.3 149.8 %all-gather.11.cloned.1.call-done = bf16[768,4,4096]{2,1,0:T(4,128)(2,1)} async-done(((bf16[48,4,4096]{2,1,0:T(4,128)(2,1)}), bf16[768,4,4096]{2,1,0:T(4,128)(2,1)}) %all-gather.11.cloned.1.call-update) | async-done | bytes 25165840 | tf_op jit(solution)/shard_map/all_gather | solution.py:12
  359.0 13.5 %reduce_sum.86 = bf16[48,4,4096]{2,1,0:T(4,128)(2,1)S(1)} reduce(bf16[16,48,4,4096]{3,2,1,0:T(4,128)(2,1)} %bitcast.70, bf16[]{:T(256)} %constant.89.clone.1), dimensions={0}, to_apply=%region_5.6 | reduce | flops 11796480 | bytes 26738690 | tf_op jit(solution)/shard_map/reduce_sum | solution.py:13
  372.6 1.8 fusion.41
  374.4 3.8 reshape.333
  378.2 1.9 reshape.335
  380.1 7.9 %fusion.3 = f32[48,4,64,64,1]{3,2,1,4,0:T(8,128)} fusion(bf16[48,2,4,64,64]{4,3,2,1,0:T(8,128)(2,1)} %reshape.251, bf16[48,2,64,64,1]{3,2,1,0,4:T(8,128)(2,1)} %reshape.333), kind=kOutput, calls=%fused_computation.10 | convolution fusion | flops 201326592 | bytes 7077888 | tf_op jit(solution)/shard_map/iqmn,iqjnp->ijmp/dot_general | solution.py:74
  388.0 6.6 %fusion.1 = bf16[48,4,64,64]{2,3,1,0:T(8,128)(2,1)} fusion(f32[48,4,64,64,1]{3,2,1,4,0:T(8,128)} %fusion.3, bf16[48,2,4,64,64]{4,3,2,1,0:T(8,128)(2,1)S(1)} %bitcast.72, bf16[48,2,64,64,1]{3,2,1,0,4:T(8,128)(2,1)S(1)} %copy-done.2), kind=kOutput, calls=%fused_computation.8 | convolution fusion | flops 202899456 | bytes 8650752 | tf_op jit(solution)/shard_map/iqmn,iqjnp->ijmp/dot_general | solution.py:74
  394.6 3.4 copy.74
  398.0 3.2 reshape.339
  (73 shorter events, 12.8 us)
Async XLA Ops:
  6.5 188.4 %all-gather.13.cloned.1.call-start = ((), (), s32[]{:S(2)}) async-start(), calls=%async_computation.1 | async-start | bytes 26738688 | tf_op jit(solution)/shard_map/all_gather | solution.py:12
  6.5 5.1 %copy-start.1 = (bf16[48,4,4096]{2,1,0:T(4,128)(2,1)S(1)}, bf16[48,4,4096]{2,1,0:T(4,128)(2,1)}, u32[]{:S(2)}) copy-start(bf16[48,4,4096]{2,1,0:T(4,128)(2,1)} %param.3) | copy-start | bytes 4718596
  6.5 18.0 %copy-start = (s32[48,1]{0,1:T(1,128)S(1)}, s32[48,1]{0,1:T(1,128)}, u32[]{:S(2)}) copy-start(s32[48,1]{0,1:T(1,128)} %param.5) | copy-start | bytes 580
  6.5 20.7 %copy-start.3 = (s32[48,4]{0,1:T(4,128)S(1)}, s32[48,4]{0,1:T(4,128)}, u32[]{:S(2)}) copy-start(s32[48,4]{0,1:T(4,128)} %param.4) | copy-start | bytes 2308
  10.9 348.1 %all-gather.11.cloned.1.call-start = ((), (), s32[]{:S(2)}) async-start(), calls=%async_computation | async-start | bytes 26738688 | tf_op jit(solution)/shard_map/all_gather | solution.py:12
  11.7 108.9 %collective-permute-start.2 = (bf16[48,4,4096]{2,1,0:T(4,128)(2,1)S(1)}, bf16[48,4,4096]{2,1,0:T(4,128)(2,1)S(1)}, u32[]{:S(2)}, u32[]{:S(2)}) collective-permute-start(bf16[48,4,4096]{2,1,0:T(4,128)(2,1)S(1)} %copy-done.1), channel_id=1, source_target_pairs={{1,0},{2,1},{3,2},{4,3},{5,4},{6,5},{7,6},{8,7},{9,8},{10,9},{11,1... | collective-permute-start | bytes 4718600 | tf_op jit(solution)/shard_map/ppermute | solution.py:25
  24.6 93.9 %collective-permute-start.1 = (s32[48]{0:T(128)S(1)}, s32[48]{0:T(128)S(1)}, u32[]{:S(2)}, u32[]{:S(2)}) collective-permute-start(s32[48]{0:T(128)S(1)} %bitcast.66), channel_id=1, source_target_pairs={{1,0},{2,1},{3,2},{4,3},{5,4},{6,5},{7,6},{8,7},{9,8},{10,9},{11,1... | collective-permute-start | bytes 584 | tf_op jit(solution)/shard_map/ppermute | solution.py:25
  27.3 92.6 %collective-permute-start = (s32[48,4]{1,0:T(8,128)S(1)}, s32[48,4]{1,0:T(8,128)S(1)}, u32[]{:S(2)}, u32[]{:S(2)}) collective-permute-start(s32[48,4]{1,0:T(8,128)S(1)} %copy.54), channel_id=1, source_target_pairs={{1,0},{2,1},{3,2},{4,3},{5,4},{6,5},{7,6},{8,7},{9,8},{10,9},{11,1... | collective-permute-start | bytes 2312 | tf_op jit(solution)/shard_map/ppermute | solution.py:25
  378.2 9.8 %slice-start = ((s8[6291456]{0:T(1024)(128)(4,1)}), s8[2097152]{0:T(1024)(128)(4,1)S(1)}, s32[]{:S(2)}) async-start(s8[6291456]{0:T(1024)(128)(4,1)} %bitcast.71), calls=%async_computation.2 | async-start | bytes 4194304
  380.1 7.9 %slice-start.1 = ((s8[6291456]{0:T(1024)(128)(4,1)}), s8[4194304]{0:T(1024)(128)(4,1)S(1)}, s32[]{:S(2)}) async-start(s8[6291456]{0:T(1024)(128)(4,1)} %bitcast.71), calls=%async_computation.3 | async-start | bytes 8388608
  380.1 7.9 %copy-start.2 = (bf16[48,2,64,64,1]{3,2,1,0,4:T(8,128)(2,1)S(1)}, bf16[48,2,64,64,1]{3,2,1,0,4:T(8,128)(2,1)}, u32[]{:S(2)}) copy-start(bf16[48,2,64,64,1]{3,2,1,0,4:T(8,128)(2,1)} %reshape.335) | copy-start | bytes 2359300
Sparse Core Ops, SparseCore 0:
  11.1 183.8 all-gather.12
  198.3 160.6 all-gather.10
